TPU v7x, 256 devices: a whole 4x4x8 slice. The times are simulated.
256 devices in a mesh: layer: 4 (over x_lo, core), space: 64 (over x_hi, y, z).
Axes of the slice: x: 4 (x_hi: 2, x_lo: 2; x = x_hi * 2 + x_lo), y: 4, z: 8, core: 2. Of those that a mesh axis runs over, the one named last changes fastest.
Arguments:
- states: bfloat16 [4, 512, 128, 256], P('layer', 'space'), may hold values from -6 to 6
- coarse_old: bfloat16 [4, 512, 128, 256], P('layer', 'space'), may hold values from -6 to 6
- fine_weights: bfloat16 [4, 3, 9, 256, 256], P('layer'), may hold values from -0.125 to 0.125
- coarse_weights: bfloat16 [4, 9, 256, 256], P('layer'), may hold values from -0.125 to 0.125
Outputs:
- end_states: bfloat16 [4, 512, 128, 256], P('layer', 'space')
- coarse_new: bfloat16 [4, 512, 128, 256], P('layer', 'space')
All inputs are finite; a program needn't handle non-finite values.
Results may differ from a plain program's by a relative error of at most 0.008.
Values may be sent and summed in bfloat16 or wider, within the bound.
A program may use at most 64 MiB of HBM per device.

v0:
```python
import jax
import jax.numpy as jnp
from jax import lax
from jax.sharding import PartitionSpec as P


def padded_2(array, sides, width):
    for axis, dim in sides:
        size, length = (lax.axis_size(axis), array.shape[dim])
        up = [(i, (i + 1) % size) for i in range(size - 1)]
        down = [(j, i) for i, j in up]
        last = lax.slice_in_dim(array, length - width, length, axis=dim)
        initial = lax.slice_in_dim(array, 0, width, axis=dim)
        before = lax.ppermute(last, axis, up)
        after = lax.ppermute(initial, axis, down)
        array = jnp.concatenate([before, array, after], axis=dim)
    return array


def from_behind(array, axis, by):
    length = lax.axis_size(axis)
    pairs = [(i, i + by) for i in range(length) if 0 <= i + by < length]
    return lax.ppermute(array, axis, pairs)


def conv_rows(padded, kernel):
    out_rows = padded.shape[0] - 2
    width_cols = padded.shape[1]
    widened = jnp.pad(padded, ((0, 0), (1, 1), (0, 0)))
    summed = jnp.zeros((out_rows, width_cols, padded.shape[2]), jnp.float32)
    for position in range(9):
        row_step, col_step = divmod(position, 3)
        window = widened[row_step : row_step + out_rows, col_step : col_step + width_cols]
        summed = summed + jnp.einsum(
            "rwc,cd->rwd", window, kernel[position], preferred_element_type=jnp.float32
        )
    return summed


def coarse_step(entering, kernel):
    padded = padded_2(entering, (("space", 0),), 1)
    return entering.astype(jnp.float32) + jax.nn.relu(conv_rows(padded, kernel))


def per_device(states, coarse_old, fine_weights, coarse_weights):
    strip_rows = states.shape[1]
    margin = fine_weights.shape[1]
    field = states[0]
    current = padded_2(field, (("space", 0),), margin)
    offset = lax.axis_index("space") * strip_rows - margin
    height_all = strip_rows * lax.axis_size("space")
    for layer_no in range(margin):
        result = current[1:-1].astype(jnp.float32) + jax.nn.relu(
            conv_rows(current, fine_weights[0, layer_no])
        )
        offset = offset + 1
        global_rows = offset + jnp.arange(result.shape[0], dtype=jnp.int32)
        inside = (global_rows >= 0) & (global_rows < height_all)
        current = jnp.where(inside[:, None, None], result, 0.0).astype(jnp.bfloat16)
    field = current
    layer_index = lax.axis_index("layer")
    group_count = lax.axis_size("layer")
    end_state = jnp.zeros_like(field)
    coarse_out = jnp.zeros_like(field)
    delta = field.astype(jnp.float32) - coarse_old[0].astype(jnp.float32)
    entering = states[0]
    for turn in range(group_count):
        coarse_val = coarse_step(entering, coarse_weights[0])
        corrected = (coarse_val + delta).astype(jnp.bfloat16)
        chosen = layer_index == turn
        end_state = jnp.where(chosen, corrected, end_state)
        coarse_out = jnp.where(chosen, coarse_val.astype(jnp.bfloat16), coarse_out)
        if turn + 1 < group_count:
            entering = from_behind(corrected, "layer", 1)
    return (end_state[None], coarse_out[None])


def solution(mesh):
    in_specs = (
        P("layer", "space", None, None),
        P("layer", "space", None, None),
        P("layer", None, None, None, None),
        P("layer", None, None, None),
    )
    out_specs = (P("layer", "space", None, None), P("layer", "space", None, None))
    return jax.shard_map(
        per_device, mesh=mesh, in_specs=in_specs, out_specs=out_specs, check_vma=False
    )
```

profile of v0, /device:TPU:6, one launch (start us, length us, event | category | flops | bytes accessed | tf_op | source)
XLA Modules:
  0.0 135.2 jit_solution(6629183840697172845)
XLA Ops:
  0.7 1.2 slice_bitcast_fusion.1
  1.8 3.8 %collective-permute-start.2 = (bf16[3,128,256]{2,1,0:T(8,128)(2,1)S(1)}, bf16[3,128,256]{2,1,0:T(8,128)(2,1)S(1)}, u32[]{:S(2)}, u32[]{:S(2)}) collective-permute-start(bf16[3,128,256]{2,1,0:T(8,128)(2,1)S(1)} %get-tuple-element.12), channel_id=1, source_target_pairs={{0,1},{1,2},{2,3},{3,4},{4,5},{5,6},{6,7},{7,8},{8,9},{9,10},{10,1... | collective-permute-start | bytes 589832 | tf_op jit(solution)/shard_map/ppermute | solution.py:14
  5.7 9.2 %collective-permute-start.3 = (bf16[3,128,256]{2,1,0:T(8,128)(2,1)S(1)}, bf16[3,128,256]{2,1,0:T(8,128)(2,1)S(1)}, u32[]{:S(2)}, u32[]{:S(2)}) collective-permute-start(bf16[3,128,256]{2,1,0:T(8,128)(2,1)S(1)} %get-tuple-element.13), channel_id=1, source_target_pairs={{1,0},{2,1},{3,2},{4,3},{5,4},{6,5},{7,6},{8,7},{9,8},{10,9},{11,1... | collective-permute-start | bytes 589832 | tf_op jit(solution)/shard_map/ppermute | solution.py:15
  14.8 0.9 slice_bitcast_fusion.3
  15.7 1.9 %collective-permute-start = (bf16[1,128,256]{2,1,0:T(8,128)(2,1)S(1)}, bf16[1,128,256]{2,1,0:T(8,128)(2,1)S(1)}, u32[]{:S(2)}, u32[]{:S(2)}) collective-permute-start(bf16[1,128,256]{2,1,0:T(8,128)(2,1)S(1)} %get-tuple-element.10), channel_id=1, source_target_pairs={{0,1},{1,2},{2,3},{3,4},{4,5},{5,6},{6,7},{7,8},{8,9},{9,10},{10,1... | collective-permute-start | bytes 196616 | tf_op jit(solution)/shard_map/ppermute | solution.py:14
  17.6 9.6 %collective-permute-start.1 = (bf16[1,128,256]{2,1,0:T(8,128)(2,1)S(1)}, bf16[1,128,256]{2,1,0:T(8,128)(2,1)S(1)}, u32[]{:S(2)}, u32[]{:S(2)}) collective-permute-start(bf16[1,128,256]{2,1,0:T(8,128)(2,1)S(1)} %get-tuple-element.11), channel_id=1, source_target_pairs={{1,0},{2,1},{3,2},{4,3},{5,4},{6,5},{7,6},{8,7},{9,8},{10,9},{11,1... | collective-permute-start | bytes 196616 | tf_op jit(solution)/shard_map/ppermute | solution.py:15
  27.6 1.6 %collective-permute-done.1 = bf16[1,128,256]{2,1,0:T(8,128)(2,1)S(1)} collective-permute-done((bf16[1,128,256]{2,1,0:T(8,128)(2,1)S(1)}, bf16[1,128,256]{2,1,0:T(8,128)(2,1)S(1)}, u32[]{:S(2)}, u32[]{:S(2)}) %collective-permute-start.1) | collective-permute-done | bytes 65568 | tf_op jit(solution)/shard_map/ppermute | solution.py:15
  32.0 1.2 copy-done.6
  33.2 0.4 fusion.35
  33.6 0.4 fusion.37
  34.0 0.4 fusion.39
  34.4 0.4 fusion.41
  34.8 0.4 fusion.43
  35.2 0.4 fusion.176
  35.5 0.4 fusion.180
  35.9 0.4 fusion.172
  36.3 0.9 select_convert_fusion
  37.9 0.4 fusion.51
  38.6 0.4 fusion
  39.4 0.4 fusion.1
  40.1 0.5 fusion.27
  42.5 0.4 fusion.20
  43.2 0.7 copy-done.14
  44.0 0.5 fusion.30
  44.5 1.2 add_convert_fusion.3
  45.7 1.9 %collective-permute-start.4 = (bf16[8,128,256]{2,1,0:T(8,128)(2,1)S(1)}, bf16[8,128,256]{2,1,0:T(8,128)(2,1)S(1)}, u32[]{:S(2)}, u32[]{:S(2)}) collective-permute-start(bf16[8,128,256]{2,1,0:T(8,128)(2,1)S(1)} %get-tuple-element.14), channel_id=1, source_target_pairs={{0,64},{64,128},{128,192},{1,65},{65,129},{129,193},{2,66},{66,130... | collective-permute-start | bytes 1572872 | tf_op jit(solution)/shard_map/ppermute | solution.py:23
  47.6 8.6 %collective-permute-done.4 = bf16[8,128,256]{2,1,0:T(8,128)(2,1)S(1)} collective-permute-done((bf16[8,128,256]{2,1,0:T(8,128)(2,1)S(1)}, bf16[8,128,256]{2,1,0:T(8,128)(2,1)S(1)}, u32[]{:S(2)}, u32[]{:S(2)}) %collective-permute-start.4) | collective-permute-done | bytes 524320 | tf_op jit(solution)/shard_map/ppermute | solution.py:23
  56.2 1.9 %collective-permute-start.5 = (bf16[1,128,256]{2,1,0:T(8,128)(2,1)S(1)}, bf16[1,128,256]{2,1,0:T(8,128)(2,1)S(1)}, u32[]{:S(2)}, u32[]{:S(2)}) collective-permute-start(bf16[1,128,256]{2,1,0:T(8,128)(2,1)S(1)} %get-tuple-element.8), channel_id=1, source_target_pairs={{0,1},{1,2},{2,3},{3,4},{4,5},{5,6},{6,7},{7,8},{8,9},{9,10},{10,1... | collective-permute-start | bytes 196616 | tf_op jit(solution)/shard_map/ppermute | solution.py:14
  58.1 10.1 %collective-permute-start.6 = (bf16[1,128,256]{2,1,0:T(8,128)(2,1)S(1)}, bf16[1,128,256]{2,1,0:T(8,128)(2,1)S(1)}, u32[]{:S(2)}, u32[]{:S(2)}) collective-permute-start(bf16[1,128,256]{2,1,0:T(8,128)(2,1)S(1)} %get-tuple-element.9), channel_id=1, source_target_pairs={{1,0},{2,1},{3,2},{4,3},{5,4},{6,5},{7,6},{8,7},{9,8},{10,9},{11,1... | collective-permute-start | bytes 196616 | tf_op jit(solution)/shard_map/ppermute | solution.py:15
  68.3 1.6 %collective-permute-done.6 = bf16[1,128,256]{2,1,0:T(8,128)(2,1)S(1)} collective-permute-done((bf16[1,128,256]{2,1,0:T(8,128)(2,1)S(1)}, bf16[1,128,256]{2,1,0:T(8,128)(2,1)S(1)}, u32[]{:S(2)}, u32[]{:S(2)}) %collective-permute-start.6) | collective-permute-done | bytes 65568 | tf_op jit(solution)/shard_map/ppermute | solution.py:15
  72.6 1.4 %add_convert_fusion.2 = (bf16[8,128,256]{2,1,0:T(8,128)(2,1)S(1)}, f32[8,128,256]{2,1,0:T(8,128)}) fusion(f32[8,128,256]{2,1,0:T(8,128)S(1)} %fusion.30, bf16[8,128,256]{2,1,0:T(8,128)(2,1)S(1)} %collective-permute-done.4, f32[8,128,256]{2,1,0:T(8,128)S(1)} %fusion.114, f32[8,128,256]{2,1,0:T(8,128)S(1)} %convolution_add_fusion.22, ...), kind=kOutput, calls=%fused_computation.71 | convolution fusion | flops 137232384 | bytes 5963776 | tf_op jit(solution)/shard_map/rwc,cd->rwd/dot_general | solution.py:34
  74.0 1.9 %collective-permute-start.7 = (bf16[8,128,256]{2,1,0:T(8,128)(2,1)S(1)}, bf16[8,128,256]{2,1,0:T(8,128)(2,1)S(1)}, u32[]{:S(2)}, u32[]{:S(2)}) collective-permute-start(bf16[8,128,256]{2,1,0:T(8,128)(2,1)S(1)} %get-tuple-element.16), channel_id=1, source_target_pairs={{0,64},{64,128},{128,192},{1,65},{65,129},{129,193},{2,66},{66,130... | collective-permute-start | bytes 1572872 | tf_op jit(solution)/shard_map/ppermute | solution.py:23
  75.9 8.6 %collective-permute-done.7 = bf16[8,128,256]{2,1,0:T(8,128)(2,1)S(1)} collective-permute-done((bf16[8,128,256]{2,1,0:T(8,128)(2,1)S(1)}, bf16[8,128,256]{2,1,0:T(8,128)(2,1)S(1)}, u32[]{:S(2)}, u32[]{:S(2)}) %collective-permute-start.7) | collective-permute-done | bytes 524320 | tf_op jit(solution)/shard_map/ppermute | solution.py:23
  84.5 1.9 %collective-permute-start.8 = (bf16[1,128,256]{2,1,0:T(8,128)(2,1)S(1)}, bf16[1,128,256]{2,1,0:T(8,128)(2,1)S(1)}, u32[]{:S(2)}, u32[]{:S(2)}) collective-permute-start(bf16[1,128,256]{2,1,0:T(8,128)(2,1)S(1)} %get-tuple-element.6), channel_id=1, source_target_pairs={{0,1},{1,2},{2,3},{3,4},{4,5},{5,6},{6,7},{7,8},{8,9},{9,10},{10,1... | collective-permute-start | bytes 196616 | tf_op jit(solution)/shard_map/ppermute | solution.py:14
  86.5 10.0 %collective-permute-start.9 = (bf16[1,128,256]{2,1,0:T(8,128)(2,1)S(1)}, bf16[1,128,256]{2,1,0:T(8,128)(2,1)S(1)}, u32[]{:S(2)}, u32[]{:S(2)}) collective-permute-start(bf16[1,128,256]{2,1,0:T(8,128)(2,1)S(1)} %get-tuple-element.7), channel_id=1, source_target_pairs={{1,0},{2,1},{3,2},{4,3},{5,4},{6,5},{7,6},{8,7},{9,8},{10,9},{11,1... | collective-permute-start | bytes 196616 | tf_op jit(solution)/shard_map/ppermute | solution.py:15
  96.8 1.6 %collective-permute-done.9 = bf16[1,128,256]{2,1,0:T(8,128)(2,1)S(1)} collective-permute-done((bf16[1,128,256]{2,1,0:T(8,128)(2,1)S(1)}, bf16[1,128,256]{2,1,0:T(8,128)(2,1)S(1)}, u32[]{:S(2)}, u32[]{:S(2)}) %collective-permute-start.9) | collective-permute-done | bytes 65568 | tf_op jit(solution)/shard_map/ppermute | solution.py:15
  101.0 1.4 %add_convert_fusion.1 = (bf16[8,128,256]{2,1,0:T(8,128)(2,1)S(1)}, f32[8,128,256]{2,1,0:T(8,128)}) fusion(f32[8,128,256]{2,1,0:T(8,128)S(1)} %fusion.30, bf16[8,128,256]{2,1,0:T(8,128)(2,1)S(1)} %collective-permute-done.7, f32[8,128,256]{2,1,0:T(8,128)S(1)} %fusion.106, f32[8,128,256]{2,1,0:T(8,128)S(1)} %convolution_add_fusion.17, ...), kind=kOutput, calls=%fused_computation.69 | convolution fusion | flops 137232384 | bytes 5963776 | tf_op jit(solution)/shard_map/rwc,cd->rwd/dot_general | solution.py:34
  102.4 1.9 %collective-permute-start.10 = (bf16[8,128,256]{2,1,0:T(8,128)(2,1)S(1)}, bf16[8,128,256]{2,1,0:T(8,128)(2,1)S(1)}, u32[]{:S(2)}, u32[]{:S(2)}) collective-permute-start(bf16[8,128,256]{2,1,0:T(8,128)(2,1)S(1)} %get-tuple-element.18), channel_id=1, source_target_pairs={{0,64},{64,128},{128,192},{1,65},{65,129},{129,193},{2,66},{66,130... | collective-permute-start | bytes 1572872 | tf_op jit(solution)/shard_map/ppermute | solution.py:23
  104.3 8.6 %collective-permute-done.10 = bf16[8,128,256]{2,1,0:T(8,128)(2,1)S(1)} collective-permute-done((bf16[8,128,256]{2,1,0:T(8,128)(2,1)S(1)}, bf16[8,128,256]{2,1,0:T(8,128)(2,1)S(1)}, u32[]{:S(2)}, u32[]{:S(2)}) %collective-permute-start.10) | collective-permute-done | bytes 524320 | tf_op jit(solution)/shard_map/ppermute | solution.py:23
  112.9 0.8 copy-done.2
  113.7 1.9 %collective-permute-start.11 = (bf16[1,128,256]{2,1,0:T(8,128)(2,1)S(1)}, bf16[1,128,256]{2,1,0:T(8,128)(2,1)S(1)}, u32[]{:S(2)}, u32[]{:S(2)}) collective-permute-start(bf16[1,128,256]{2,1,0:T(8,128)(2,1)S(1)} %get-tuple-element.4), channel_id=1, source_target_pairs={{0,1},{1,2},{2,3},{3,4},{4,5},{5,6},{6,7},{7,8},{8,9},{9,10},{10,1... | collective-permute-start | bytes 196616 | tf_op jit(solution)/shard_map/ppermute | solution.py:14
  115.7 10.0 %collective-permute-start.12 = (bf16[1,128,256]{2,1,0:T(8,128)(2,1)S(1)}, bf16[1,128,256]{2,1,0:T(8,128)(2,1)S(1)}, u32[]{:S(2)}, u32[]{:S(2)}) collective-permute-start(bf16[1,128,256]{2,1,0:T(8,128)(2,1)S(1)} %get-tuple-element.5), channel_id=1, source_target_pairs={{1,0},{2,1},{3,2},{4,3},{5,4},{6,5},{7,6},{8,7},{9,8},{10,9},{11,1... | collective-permute-start | bytes 196616 | tf_op jit(solution)/shard_map/ppermute | solution.py:15
  125.9 1.6 %collective-permute-done.12 = bf16[1,128,256]{2,1,0:T(8,128)(2,1)S(1)} collective-permute-done((bf16[1,128,256]{2,1,0:T(8,128)(2,1)S(1)}, bf16[1,128,256]{2,1,0:T(8,128)(2,1)S(1)}, u32[]{:S(2)}, u32[]{:S(2)}) %collective-permute-start.12) | collective-permute-done | bytes 65568 | tf_op jit(solution)/shard_map/ppermute | solution.py:15
  127.5 1.2 select_maximum_fusion
  129.4 0.4 copy-done.3
  131.7 0.4 copy-done.10
  132.4 0.4 copy-done.4
  133.3 1.9 %fusion.93 = (bf16[1,8,128,256]{3,2,1,0:T(8,128)(2,1)}, bf16[1,8,128,256]{3,2,1,0:T(8,128)(2,1)}) fusion(bf16[8,128,256]{2,1,0:T(8,128)(2,1)S(1)} %copy-done.3, f32[8,128,256]{2,1,0:T(8,128)S(1)} %copy-done.5, bf16[8,128,256]{2,1,0:T(8,128)(2,1)S(1)} %collective-permute-done.7, f32[8,128,256]{2,1,0:T(8,128)S(1)} %copy-done.4, ...), kind=kOutput, calls=%fused_computation.143 | convolution fusion | flops 141164544 | bytes 10682372 | tf_op jit(solution)/shard_map/rwc,cd->rwd/dot_general | solution.py:34
  (84 shorter events, 16.2 us)
Async XLA Ops:
  0.6 28.5 %copy-start = (bf16[1,8,128,256]{3,2,1,0:T(8,128)(2,1)S(1)}, bf16[1,8,128,256]{3,2,1,0:T(8,128)(2,1)}, u32[]{:S(2)}) copy-start(bf16[1,8,128,256]{3,2,1,0:T(8,128)(2,1)} %param.4) | copy-start | bytes 1572868
  0.6 28.7 %copy-start.1 = (bf16[1,9,256,256]{3,2,1,0:T(8,128)(2,1)S(1)}, bf16[1,9,256,256]{3,2,1,0:T(8,128)(2,1)}, u32[]{:S(2)}) copy-start(bf16[1,9,256,256]{3,2,1,0:T(8,128)(2,1)} %param.7) | copy-start | bytes 3538948
  1.8 30.0 %collective-permute-start.2 = (bf16[3,128,256]{2,1,0:T(8,128)(2,1)S(1)}, bf16[3,128,256]{2,1,0:T(8,128)(2,1)S(1)}, u32[]{:S(2)}, u32[]{:S(2)}) collective-permute-start(bf16[3,128,256]{2,1,0:T(8,128)(2,1)S(1)} %get-tuple-element.12), channel_id=1, source_target_pairs={{0,1},{1,2},{2,3},{3,4},{4,5},{5,6},{6,7},{7,8},{8,9},{9,10},{10,1... | collective-permute-start | bytes 589832 | tf_op jit(solution)/shard_map/ppermute | solution.py:14
  5.7 26.2 %collective-permute-start.3 = (bf16[3,128,256]{2,1,0:T(8,128)(2,1)S(1)}, bf16[3,128,256]{2,1,0:T(8,128)(2,1)S(1)}, u32[]{:S(2)}, u32[]{:S(2)}) collective-permute-start(bf16[3,128,256]{2,1,0:T(8,128)(2,1)S(1)} %get-tuple-element.13), channel_id=1, source_target_pairs={{1,0},{2,1},{3,2},{4,3},{5,4},{6,5},{7,6},{8,7},{9,8},{10,9},{11,1... | collective-permute-start | bytes 589832 | tf_op jit(solution)/shard_map/ppermute | solution.py:15
  15.7 11.9 %collective-permute-start = (bf16[1,128,256]{2,1,0:T(8,128)(2,1)S(1)}, bf16[1,128,256]{2,1,0:T(8,128)(2,1)S(1)}, u32[]{:S(2)}, u32[]{:S(2)}) collective-permute-start(bf16[1,128,256]{2,1,0:T(8,128)(2,1)S(1)} %get-tuple-element.10), channel_id=1, source_target_pairs={{0,1},{1,2},{2,3},{3,4},{4,5},{5,6},{6,7},{7,8},{8,9},{9,10},{10,1... | collective-permute-start | bytes 196616 | tf_op jit(solution)/shard_map/ppermute | solution.py:14
  17.6 11.5 %collective-permute-start.1 = (bf16[1,128,256]{2,1,0:T(8,128)(2,1)S(1)}, bf16[1,128,256]{2,1,0:T(8,128)(2,1)S(1)}, u32[]{:S(2)}, u32[]{:S(2)}) collective-permute-start(bf16[1,128,256]{2,1,0:T(8,128)(2,1)S(1)} %get-tuple-element.11), channel_id=1, source_target_pairs={{1,0},{2,1},{3,2},{4,3},{5,4},{6,5},{7,6},{8,7},{9,8},{10,9},{11,1... | collective-permute-start | bytes 196616 | tf_op jit(solution)/shard_map/ppermute | solution.py:15
  31.2 2.0 %copy-start.6 = (bf16[1,3,9,256,256]{4,3,2,1,0:T(8,128)(2,1)S(1)}, bf16[1,3,9,256,256]{4,3,2,1,0:T(8,128)(2,1)}, u32[]{:S(2)}) copy-start(bf16[1,3,9,256,256]{4,3,2,1,0:T(8,128)(2,1)} %param.6) | copy-start | bytes 10616836
  42.9 1.0 copy-start.14
  45.7 24.3 %copy-start.11 = (bf16[8,128,256]{2,1,0:T(8,128)(2,1)}, bf16[8,128,256]{2,1,0:T(8,128)(2,1)S(1)}, u32[]{:S(2)}) copy-start(bf16[8,128,256]{2,1,0:T(8,128)(2,1)S(1)} %get-tuple-element.14) | copy-start | bytes 1572868
  45.7 10.5 %collective-permute-start.4 = (bf16[8,128,256]{2,1,0:T(8,128)(2,1)S(1)}, bf16[8,128,256]{2,1,0:T(8,128)(2,1)S(1)}, u32[]{:S(2)}, u32[]{:S(2)}) collective-permute-start(bf16[8,128,256]{2,1,0:T(8,128)(2,1)S(1)} %get-tuple-element.14), channel_id=1, source_target_pairs={{0,64},{64,128},{128,192},{1,65},{65,129},{129,193},{2,66},{66,130... | collective-permute-start | bytes 1572872 | tf_op jit(solution)/shard_map/ppermute | solution.py:23
  56.2 12.2 %collective-permute-start.5 = (bf16[1,128,256]{2,1,0:T(8,128)(2,1)S(1)}, bf16[1,128,256]{2,1,0:T(8,128)(2,1)S(1)}, u32[]{:S(2)}, u32[]{:S(2)}) collective-permute-start(bf16[1,128,256]{2,1,0:T(8,128)(2,1)S(1)} %get-tuple-element.8), channel_id=1, source_target_pairs={{0,1},{1,2},{2,3},{3,4},{4,5},{5,6},{6,7},{7,8},{8,9},{9,10},{10,1... | collective-permute-start | bytes 196616 | tf_op jit(solution)/shard_map/ppermute | solution.py:14
  58.1 11.8 %collective-permute-start.6 = (bf16[1,128,256]{2,1,0:T(8,128)(2,1)S(1)}, bf16[1,128,256]{2,1,0:T(8,128)(2,1)S(1)}, u32[]{:S(2)}, u32[]{:S(2)}) collective-permute-start(bf16[1,128,256]{2,1,0:T(8,128)(2,1)S(1)} %get-tuple-element.9), channel_id=1, source_target_pairs={{1,0},{2,1},{3,2},{4,3},{5,4},{6,5},{7,6},{8,7},{9,8},{10,9},{11,1... | collective-permute-start | bytes 196616 | tf_op jit(solution)/shard_map/ppermute | solution.py:15
  74.0 24.8 %copy-start.7 = (bf16[8,128,256]{2,1,0:T(8,128)(2,1)}, bf16[8,128,256]{2,1,0:T(8,128)(2,1)S(1)}, u32[]{:S(2)}) copy-start(bf16[8,128,256]{2,1,0:T(8,128)(2,1)S(1)} %get-tuple-element.16) | copy-start | bytes 1572868
  74.0 10.5 %collective-permute-start.7 = (bf16[8,128,256]{2,1,0:T(8,128)(2,1)S(1)}, bf16[8,128,256]{2,1,0:T(8,128)(2,1)S(1)}, u32[]{:S(2)}, u32[]{:S(2)}) collective-permute-start(bf16[8,128,256]{2,1,0:T(8,128)(2,1)S(1)} %get-tuple-element.16), channel_id=1, source_target_pairs={{0,64},{64,128},{128,192},{1,65},{65,129},{129,193},{2,66},{66,130... | collective-permute-start | bytes 1572872 | tf_op jit(solution)/shard_map/ppermute | solution.py:23
  84.5 12.2 %collective-permute-start.8 = (bf16[1,128,256]{2,1,0:T(8,128)(2,1)S(1)}, bf16[1,128,256]{2,1,0:T(8,128)(2,1)S(1)}, u32[]{:S(2)}, u32[]{:S(2)}) collective-permute-start(bf16[1,128,256]{2,1,0:T(8,128)(2,1)S(1)} %get-tuple-element.6), channel_id=1, source_target_pairs={{0,1},{1,2},{2,3},{3,4},{4,5},{5,6},{6,7},{7,8},{8,9},{9,10},{10,1... | collective-permute-start | bytes 196616 | tf_op jit(solution)/shard_map/ppermute | solution.py:14
  86.5 11.9 %collective-permute-start.9 = (bf16[1,128,256]{2,1,0:T(8,128)(2,1)S(1)}, bf16[1,128,256]{2,1,0:T(8,128)(2,1)S(1)}, u32[]{:S(2)}, u32[]{:S(2)}) collective-permute-start(bf16[1,128,256]{2,1,0:T(8,128)(2,1)S(1)} %get-tuple-element.7), channel_id=1, source_target_pairs={{1,0},{2,1},{3,2},{4,3},{5,4},{6,5},{7,6},{8,7},{9,8},{10,9},{11,1... | collective-permute-start | bytes 196616 | tf_op jit(solution)/shard_map/ppermute | solution.py:15
  102.4 11.3 %copy-start.9 = (bf16[8,128,256]{2,1,0:T(8,128)(2,1)}, bf16[8,128,256]{2,1,0:T(8,128)(2,1)S(1)}, u32[]{:S(2)}) copy-start(bf16[8,128,256]{2,1,0:T(8,128)(2,1)S(1)} %get-tuple-element.18) | copy-start | bytes 1572868
  102.4 10.5 %collective-permute-start.10 = (bf16[8,128,256]{2,1,0:T(8,128)(2,1)S(1)}, bf16[8,128,256]{2,1,0:T(8,128)(2,1)S(1)}, u32[]{:S(2)}, u32[]{:S(2)}) collective-permute-start(bf16[8,128,256]{2,1,0:T(8,128)(2,1)S(1)} %get-tuple-element.18), channel_id=1, source_target_pairs={{0,64},{64,128},{128,192},{1,65},{65,129},{129,193},{2,66},{66,130... | collective-permute-start | bytes 1572872 | tf_op jit(solution)/shard_map/ppermute | solution.py:23
  112.9 0.8 copy-start.2
  113.7 12.2 %collective-permute-start.11 = (bf16[1,128,256]{2,1,0:T(8,128)(2,1)S(1)}, bf16[1,128,256]{2,1,0:T(8,128)(2,1)S(1)}, u32[]{:S(2)}, u32[]{:S(2)}) collective-permute-start(bf16[1,128,256]{2,1,0:T(8,128)(2,1)S(1)} %get-tuple-element.4), channel_id=1, source_target_pairs={{0,1},{1,2},{2,3},{3,4},{4,5},{5,6},{6,7},{7,8},{8,9},{9,10},{10,1... | collective-permute-start | bytes 196616 | tf_op jit(solution)/shard_map/ppermute | solution.py:14
  115.7 11.9 %collective-permute-start.12 = (bf16[1,128,256]{2,1,0:T(8,128)(2,1)S(1)}, bf16[1,128,256]{2,1,0:T(8,128)(2,1)S(1)}, u32[]{:S(2)}, u32[]{:S(2)}) collective-permute-start(bf16[1,128,256]{2,1,0:T(8,128)(2,1)S(1)} %get-tuple-element.5), channel_id=1, source_target_pairs={{1,0},{2,1},{3,2},{4,3},{5,4},{6,5},{7,6},{8,7},{9,8},{10,9},{11,1... | collective-permute-start | bytes 196616 | tf_op jit(solution)/shard_map/ppermute | solution.py:15
  128.8 1.0 copy-start.3
  131.0 1.0 copy-start.10
  131.0 1.2 copy-start.12
  131.0 1.3 copy-start.13
  131.4 1.4 %copy-start.4 = (f32[8,128,256]{2,1,0:T(8,128)S(1)}, f32[8,128,256]{2,1,0:T(8,128)}, u32[]{:S(2)}) copy-start(f32[8,128,256]{2,1,0:T(8,128)} %get-tuple-element.17) | copy-start | bytes 3145732
  131.4 1.8 %copy-start.5 = (f32[8,128,256]{2,1,0:T(8,128)S(1)}, f32[8,128,256]{2,1,0:T(8,128)}, u32[]{:S(2)}) copy-start(f32[8,128,256]{2,1,0:T(8,128)} %get-tuple-element.19) | copy-start | bytes 3145732
  131.4 1.9 %copy-start.8 = (bf16[8,128,256]{2,1,0:T(8,128)(2,1)S(1)}, bf16[8,128,256]{2,1,0:T(8,128)(2,1)}, u32[]{:S(2)}) copy-start(bf16[8,128,256]{2,1,0:T(8,128)(2,1)} %copy-done.7) | copy-start | bytes 1572868
where the time goes:
time: 136 us; the launch traced here: 135 us
  starting transfers between devices  66.1 us (49%)
  waiting for transfers between devices  33 us (24%)
  matrix products  26.1 us (19%)
  local copies, waits for them, and re-layouts  6.84 us (5%)
  other arithmetic  1.89 us (1%)
    ppermute x5, starting transfers between devices, padded_2(): after = lax.ppermute(initial, axis, down)  48.9 us
    dot_general x63, matrix products, conv_rows(): jnp.einsum('rwc,cd->rwd', window, kernel[position], preferred_element_typ...  26.1 us
    ppermute x3, waiting for transfers between devices, from_behind(): return lax.ppermute(array, axis, pairs)  25.7 us
    ppermute x5, starting transfers between devices, padded_2(): before = lax.ppermute(last, axis, up)  11.5 us
    ppermute x5, waiting for transfers between devices, padded_2(): after = lax.ppermute(initial, axis, down)  6.33 us
    ppermute x3, starting transfers between devices, from_behind(): return lax.ppermute(array, axis, pairs)  5.73 us
    unnamed x30, local copies, waits for them, and re-layouts  4.76 us
  transfers between devices with their start and end apart: 13, of which 11 were waited for; matrix products, arithmetic and copies ran while one was open for 3% of the time, Pallas kernels for 0%

commit v1 on v0

v1 whole, which is shorter than its diff:
```python
import jax
import jax.numpy as jnp
from jax import lax
from jax.experimental import pallas as pl
from jax.experimental.pallas import tpu as pltpu
from jax.sharding import PartitionSpec as P

MESH = pl.DeviceIdType.MESH

RIM = 6
TOP, BOTTOM = RIM + 3, RIM + 4
LAG = (0, 2, 5, 4)


def pair_conv(read, weights, pair):
    taps = []
    for row_step in (-1, 0, 1):
        taps.append(
            jnp.concatenate(
                [read(TOP - pair + row_step), read(BOTTOM + pair + row_step)], axis=0
            )
        )
    window = jnp.concatenate(taps, axis=1)
    cols = taps[0].shape[0] // 2
    rows, chans = taps[0].shape
    parts = [
        jnp.dot(
            window,
            weights[step].reshape(3 * chans, chans),
            preferred_element_type=jnp.float32,
        )
        for step in range(3)
    ]
    col = lax.broadcasted_iota(jnp.int32, (rows, chans), 0) % cols
    left = jnp.where(col == 0, 0.0, pltpu.roll(parts[0], 1, 0))
    right = jnp.where(col == cols - 1, 0.0, pltpu.roll(parts[2], rows - 1, 0))
    total = parts[1] + left + right
    return taps[1].astype(jnp.float32) + jnp.maximum(total, 0.0)


def kernel(
    states, coarse_old, fine_w, coarse_w, end_out, coarse_out,
    field, level1, level2, fine, end, cold, weights,
    load_sem, weight_sem, halo_send, halo_recv, cold_send, cold_recv,
    end_send, end_recv,
):
    layer, space = lax.axis_index("layer"), lax.axis_index("space")
    groups, strips = lax.axis_size("layer"), lax.axis_size("space")
    cols = states.shape[2]
    has_above, has_below = space > 0, space < strips - 1
    has_prev, has_next = layer > 0, layer < groups - 1
    last = groups - 1 - layer + 3

    barrier = pltpu.get_barrier_semaphore()
    peers = (
        (has_above, (layer, space - 1)),
        (has_below, (layer, space + 1)),
        (has_prev, (layer - 1, space)),
        (has_next, (layer + 1, space)),
    )
    for present, peer in peers:
        @pl.when(present)
        def _(peer=peer):
            pl.semaphore_signal(barrier, inc=1, device_id=peer, device_id_type=MESH)

    greeted = sum(present.astype(jnp.int32) for present, _ in peers)

    load_field = pltpu.make_async_copy(
        states.at[0], field.at[0, pl.ds(RIM, 8)], load_sem.at[0]
    )
    load_field.start()
    loads = []
    for which in range(4):
        source = coarse_w if which == 3 else fine_w.at[0, which]
        source = source.at[0] if which == 3 else source
        loads.append(
            [
                pltpu.make_async_copy(
                    source.at[:, step], weights.at[which, step], weight_sem.at[which, step]
                )
                for step in range(3)
            ]
        )
    for group in loads[:3]:
        for copy in group:
            copy.start()
    load_cold = pltpu.make_async_copy(
        coarse_old.at[0], cold.at[pl.ds(RIM, 8)], load_sem.at[1]
    )
    for copy in loads[3]:
        copy.start()
    load_cold.start()

    def halo(ring, side, array, target, send, recv):
        row = 8 - ring if side == 0 else ring - 1
        slot = RIM - ring if side == 0 else RIM + 7 + ring
        return pltpu.make_async_remote_copy(
            src_ref=array.at[0, row],
            dst_ref=target.at[slot],
            send_sem=send.at[side, ring - 1],
            recv_sem=recv.at[side, ring - 1],
            device_id=(layer, space + 1 if side == 0 else space - 1),
            device_id_type=MESH,
        )

    def field_halo(ring, side):
        return halo(ring, side, states, field.at[0], halo_send, halo_recv)

    def cold_halo(ring, side):
        return halo(ring, side, coarse_old, cold, cold_send, cold_recv)

    def end_copy(pair, side):
        slot = TOP - pair if side == 0 else BOTTOM + pair
        return pltpu.make_async_remote_copy(
            src_ref=end.at[slot],
            dst_ref=field.at[1, slot],
            send_sem=end_send.at[side, pair],
            recv_sem=end_recv.at[side, pair],
            device_id=(layer + 1, space),
            device_id_type=MESH,
        )

    to, come = (has_below, has_above), (has_above, has_below)

    def keep(pair, value):
        top, bottom = value[:cols], value[cols:]
        top_in = has_above | (pair <= 3)
        bottom_in = has_below | (pair <= 3)
        return (
            jnp.where(top_in, top, 0.0).astype(jnp.bfloat16),
            jnp.where(bottom_in, bottom, 0.0).astype(jnp.bfloat16),
        )

    def fine_step(source, target, which, pair):
        value = pair_conv(lambda row: source[row], weights[which], pair)
        target[TOP - pair], target[BOTTOM + pair] = keep(pair, value)

    @pl.when(jnp.logical_not(has_above))
    def _():
        field[0, 0:RIM] = jnp.zeros((RIM, *field.shape[2:]), field.dtype)

    @pl.when(jnp.logical_not(has_below))
    def _():
        field[0, RIM + 8 :] = jnp.zeros((RIM, *field.shape[2:]), field.dtype)

    level0 = field.at[0]
    late = has_above & (space % 8 == 0)

    def prelude(part, carry):
        @pl.when((part == 0) != late)
        def _():
            pl.semaphore_wait(barrier, greeted)

            for side in (0, 1):
                @pl.when(to[side])
                def _(side=side):
                    @pl.loop(1, last + 1)
                    def _(ring):
                        field_halo(ring, side).start()

                    @pl.loop(1, last - 2)
                    def _(ring):
                        cold_halo(ring, side).start()

        @pl.when((part == 0) == late)
        def _():
            load_field.wait()
            for copy in loads[0]:
                copy.wait()
            fine_step(level0, level1, 0, 0)
            fine_step(level0, level1, 0, 1)
            for copy in loads[1]:
                copy.wait()
            fine_step(level1, level2, 1, 0)
            for copy in loads[2] + loads[3]:
                copy.wait()
            load_cold.wait()

        return carry

    lax.fori_loop(0, 2, prelude, 0)

    source_at = jnp.where(has_prev, 1, 0)
    lag = jnp.where(layer == 0, LAG[0], jnp.where(layer == 1, LAG[1], jnp.where(layer == 2, LAG[2], LAG[3])))

    def coarse_pair(pair):
        @pl.when(pair >= 4)
        def _():
            for side in (0, 1):
                @pl.when(come[side])
                def _(side=side):
                    cold_halo(pair - 3, side).wait_recv()

        @pl.when(has_prev)
        def _():
            @pl.when(pair == 0)
            def _():
                for side in (0, 1):
                    end_copy(0, side).wait_recv()

            for side in (0, 1):
                end_copy(pair + 1, side).wait_recv()

        entering = field.at[source_at]
        value = pair_conv(lambda row: entering[row], weights[3], pair)

        def both(ref):
            rows = jnp.concatenate([ref[TOP - pair], ref[BOTTOM + pair]], axis=0)
            return rows.astype(jnp.float32)

        leaving = keep(pair, value + (both(fine) - both(cold)))
        end[TOP - pair], end[BOTTOM + pair] = leaving

        @pl.when(has_next)
        def _():
            for side in (0, 1):
                end_copy(pair, side).start()

        @pl.when(pair <= 3)
        def _():
            end_out[0, 3 - pair], end_out[0, 4 + pair] = leaving
            coarse_out[0, 3 - pair] = value[:cols].astype(jnp.bfloat16)
            coarse_out[0, 4 + pair] = value[cols:].astype(jnp.bfloat16)

    @pl.loop(0, last + 1 + lag)
    def _(turn):
        @pl.when(turn <= last)
        def _():
            @pl.when(turn >= 1)
            def _():
                for side in (0, 1):
                    @pl.when(come[side])
                    def _(side=side):
                        field_halo(turn, side).wait_recv()

            fine_step(level0, level1, 0, turn + 2)
            fine_step(level1, level2, 1, turn + 1)
            fine_step(level2, fine, 2, turn)

        @pl.when(turn >= lag)
        def _():
            coarse_pair(turn - lag)

    for side in (0, 1):
        @pl.when(to[side])
        def _(side=side):
            @pl.loop(1, last + 1)
            def _(ring):
                field_halo(ring, side).wait_send()

            @pl.loop(1, last - 2)
            def _(ring):
                cold_halo(ring, side).wait_send()

        @pl.when(has_next)
        def _(side=side):
            @pl.loop(0, last + 1)
            def _(pair):
                end_copy(pair, side).wait_send()


def per_device(states, coarse_old, fine_weights, coarse_weights):
    _, rows, cols, chans = states.shape
    out = jax.ShapeDtypeStruct(states.shape, states.dtype)
    image = (rows + 2 * RIM, cols, chans)
    bf16 = jnp.bfloat16
    dma = pltpu.SemaphoreType.DMA
    return pl.pallas_call(
        kernel,
        out_shape=(out, out),
        in_specs=[pl.BlockSpec(memory_space=pl.ANY)] * 4,
        out_specs=[pl.BlockSpec(memory_space=pltpu.VMEM)] * 2,
        scratch_shapes=[
            pltpu.VMEM((2, *image), bf16),
            pltpu.VMEM(image, bf16),
            pltpu.VMEM(image, bf16),
            pltpu.VMEM(image, bf16),
            pltpu.VMEM(image, bf16),
            pltpu.VMEM(image, bf16),
            pltpu.VMEM((4, 3, 3, chans, chans), bf16),
            dma((2,)),
            dma((4, 3)),
            dma((2, 6)),
            dma((2, 6)),
            dma((2, 3)),
            dma((2, 3)),
            dma((2, 7)),
            dma((2, 7)),
        ],
        compiler_params=pltpu.CompilerParams(
            vmem_limit_bytes=56 << 20, collective_id=0, has_side_effects=True
        ),
    )(
        states,
        coarse_old,
        fine_weights.reshape(1, 3, 3, 3, chans, chans),
        coarse_weights.reshape(1, 3, 3, chans, chans),
    )


def solution(mesh):
    in_specs = (
        P("layer", "space", None, None),
        P("layer", "space", None, None),
        P("layer", None, None, None, None),
        P("layer", None, None, None),
    )
    out_specs = (P("layer", "space", None, None), P("layer", "space", None, None))
    return jax.shard_map(
        per_device, mesh=mesh, in_specs=in_specs, out_specs=out_specs, check_vma=False
    )
```

time: 136 us -> 39.6 us (0.29)
  the two profiles are of different devices: /device:TPU:6 before, /device:TPU:7 now
where the time goes in v1:
time: 39.6 us; the launch traced here: 39.4 us
  Pallas kernels  35 us (88%)
  local copies, waits for them, and re-layouts  3.74 us (9%)
  between operations  0.64 us (2%)
    pallas_call x1, Pallas kernels, per_device(): pl.pallas_call(kernel, out_shape=(out, out), in_specs=[pl.BlockSpec(memor...  35 us
    unnamed x2, local copies, waits for them, and re-layouts  3.74 us

profile of v1, /device:TPU:7, one launch (start us, length us, event | category | flops | bytes accessed | tf_op | source)
XLA Modules:
  0.0 39.4 jit_solution(7747517696635239056)
XLA Ops:
  0.6 35.0 %shard_map.59 = (bf16[1,8,128,256]{3,2,1,0:T(8,128)(2,1)}, bf16[1,8,128,256]{3,2,1,0:T(8,128)(2,1)}) custom-call(bf16[1,8,128,256]{3,2,1,0:T(8,128)(2,1)} %states.1, bf16[1,8,128,256]{3,2,1,0:T(8,128)(2,1)} %coarse_old.1, bf16[1,3,3,3,256,256]{5,4,3,2,1,0:T(8,128)(2,1)} %bitcast.2, bf16[1,3,3,256,256]{4,3,2,1,0:T(8,128)(2,1)} %bitcast.3), custom_call_target="tpu_custom_call" | custom-call | tf_op jit(solution)/shard_map/pallas_call | solution.py:268
  35.7 1.9 %copy.8 = bf16[1,8,128,256]{3,2,1,0:T(8,128)(2,1)} copy(bf16[1,8,128,256]{3,2,1,0:T(8,128)(2,1)} %get-tuple-element.4) | data formatting | bytes 1048576
  37.5 1.9 %copy.9 = bf16[1,8,128,256]{3,2,1,0:T(8,128)(2,1)} copy(bf16[1,8,128,256]{3,2,1,0:T(8,128)(2,1)} %get-tuple-element.5) | data formatting | bytes 1048576

commit v2 on v1

--- a/solution.py
+++ b/solution.py
@@ -9,20 +9,17 @@
 
 RIM = 6
 TOP, BOTTOM = RIM + 3, RIM + 4
-LAG = (0, 2, 5, 4)
-
-
-def pair_conv(read, weights, pair):
-    taps = []
-    for row_step in (-1, 0, 1):
-        taps.append(
-            jnp.concatenate(
-                [read(TOP - pair + row_step), read(BOTTOM + pair + row_step)], axis=0
-            )
-        )
+LAG = 2
+
+
+def conv_relu(source, weights, start, count):
+    _, cols, chans = source.shape
+    rows = count * cols
+    taps = [
+        source[pl.ds(start + row_step, count)].reshape(rows, chans)
+        for row_step in (-1, 0, 1)
+    ]
     window = jnp.concatenate(taps, axis=1)
-    cols = taps[0].shape[0] // 2
-    rows, chans = taps[0].shape
     parts = [
         jnp.dot(
             window,
@@ -91,15 +88,19 @@
         copy.start()
     load_cold.start()
 
+    def pick(side, upper, lower):
+        return jnp.where(side == 0, upper, lower)
+
+    def slot_of(pair, side):
+        return pick(side, TOP - pair, BOTTOM + pair)
+
     def halo(ring, side, array, target, send, recv):
-        row = 8 - ring if side == 0 else ring - 1
-        slot = RIM - ring if side == 0 else RIM + 7 + ring
         return pltpu.make_async_remote_copy(
-            src_ref=array.at[0, row],
-            dst_ref=target.at[slot],
+            src_ref=array.at[0, pick(side, 8 - ring, ring - 1)],
+            dst_ref=target.at[slot_of(3 + ring, side)],
             send_sem=send.at[side, ring - 1],
             recv_sem=recv.at[side, ring - 1],
-            device_id=(layer, space + 1 if side == 0 else space - 1),
+            device_id=(layer, pick(side, space + 1, space - 1)),
             device_id_type=MESH,
         )
 
@@ -110,7 +111,7 @@
         return halo(ring, side, coarse_old, cold, cold_send, cold_recv)
 
     def end_copy(pair, side):
-        slot = TOP - pair if side == 0 else BOTTOM + pair
+        slot = slot_of(pair, side)
         return pltpu.make_async_remote_copy(
             src_ref=end.at[slot],
             dst_ref=field.at[1, slot],
@@ -120,20 +121,16 @@
             device_id_type=MESH,
         )
 
-    to, come = (has_below, has_above), (has_above, has_below)
-
-    def keep(pair, value):
-        top, bottom = value[:cols], value[cols:]
-        top_in = has_above | (pair <= 3)
-        bottom_in = has_below | (pair <= 3)
-        return (
-            jnp.where(top_in, top, 0.0).astype(jnp.bfloat16),
-            jnp.where(bottom_in, bottom, 0.0).astype(jnp.bfloat16),
-        )
-
-    def fine_step(source, target, which, pair):
-        value = pair_conv(lambda row: source[row], weights[which], pair)
-        target[TOP - pair], target[BOTTOM + pair] = keep(pair, value)
+    to = (has_below, has_above)
+
+    def store(target, start, count, value):
+        target[pl.ds(start, count)] = value.reshape(count, cols, -1).astype(target.dtype)
+
+    def fine_rows(source, target, which, start, count):
+        store(target, start, count, conv_relu(source, weights[which], start, count))
+
+    def in_image(pair, side):
+        return pick(side, has_above, has_below) | (pair <= 3)
 
     @pl.when(jnp.logical_not(has_above))
     def _():
@@ -144,6 +141,8 @@
         field[0, RIM + 8 :] = jnp.zeros((RIM, *field.shape[2:]), field.dtype)
 
     level0 = field.at[0]
+    late_above = has_above & (space % 8 <= 1) & (space > 1)
+    late_below = has_below & (space % 8 == 7)
     late = has_above & (space % 8 == 0)
 
     def prelude(part, carry):
@@ -167,12 +166,16 @@
             load_field.wait()
             for copy in loads[0]:
                 copy.wait()
-            fine_step(level0, level1, 0, 0)
-            fine_step(level0, level1, 0, 1)
+            for row in (1, 3, 5):
+                fine_rows(level0, level1, 0, RIM + row, 2)
             for copy in loads[1]:
                 copy.wait()
-            fine_step(level1, level2, 1, 0)
-            for copy in loads[2] + loads[3]:
+            for row in (2, 4):
+                fine_rows(level1, level2, 1, RIM + row, 2)
+            for copy in loads[2]:
+                copy.wait()
+            fine_rows(level2, fine, 2, RIM + 3, 2)
+            for copy in loads[3]:
                 copy.wait()
             load_cold.wait()
 
@@ -180,66 +183,128 @@
 
     lax.fori_loop(0, 2, prelude, 0)
 
+    apart = late_above | late_below
+    late_side = late_below.astype(jnp.int32)
+    halves = jnp.where(apart, 2, 1)
+
+    def row_of(q):
+        return jnp.where(q >= 0, q, -1 - q), jnp.where(q >= 0, late_side, 1 - late_side)
+
+    def fine_at(half, step):
+        _, side = row_of(jnp.where(half == 0, -1, 0))
+        pair = jnp.where(apart, step, step // 2) + 1
+        return pair, jnp.where(apart, side, step % 2)
+
+    def coarse_q(half, step):
+        return jnp.where(half == 0, -layer - step, step - layer + 1)
+
+    def coarse_at(half, step):
+        pair, side = row_of(coarse_q(half, step))
+        return jnp.where(apart, pair, step // 2), jnp.where(apart, side, step % 2)
+
+    def fine_step(source, target, which, pair, side):
+        slot = slot_of(pair, side)
+        value = conv_relu(source, weights[which], slot, 1)
+        store(target, slot, 1, jnp.where(in_image(pair, side), value, 0.0))
+
+    def await_ring(half, step):
+        ring, side = fine_at(half, step)
+
+        @pl.when(pick(side, has_above, has_below))
+        def _():
+            field_halo(ring, side).wait_recv()
+
+    def fine_turn(half, step):
+        pair, side = fine_at(half, step)
+        fine_step(level0, level1, 0, pair + 2, side)
+        fine_step(level1, level2, 1, pair + 1, side)
+        fine_step(level2, fine, 2, pair, side)
+
     source_at = jnp.where(has_prev, 1, 0)
-    lag = jnp.where(layer == 0, LAG[0], jnp.where(layer == 1, LAG[1], jnp.where(layer == 2, LAG[2], LAG[3])))
-
-    def coarse_pair(pair):
-        @pl.when(pair >= 4)
-        def _():
-            for side in (0, 1):
-                @pl.when(come[side])
-                def _(side=side):
-                    cold_halo(pair - 3, side).wait_recv()
-
-        @pl.when(has_prev)
-        def _():
-            @pl.when(pair == 0)
+    def await_end(pair, side):
+        end_copy(pair, side).wait_recv()
+
+    def await_entering(half, step):
+        pair, side = coarse_at(half, step)
+
+        @pl.when((pair >= 4) & pick(side, has_above, has_below))
+        def _():
+            cold_halo(pair - 3, side).wait_recv()
+
+        first = (half == 0) & (step == 0)
+
+        @pl.when(has_prev & apart)
+        def _():
+            q = coarse_q(half, step)
+
+            @pl.when(first)
             def _():
-                for side in (0, 1):
-                    end_copy(0, side).wait_recv()
-
-            for side in (0, 1):
-                end_copy(pair + 1, side).wait_recv()
-
-        entering = field.at[source_at]
-        value = pair_conv(lambda row: entering[row], weights[3], pair)
-
-        def both(ref):
-            rows = jnp.concatenate([ref[TOP - pair], ref[BOTTOM + pair]], axis=0)
-            return rows.astype(jnp.float32)
-
-        leaving = keep(pair, value + (both(fine) - both(cold)))
-        end[TOP - pair], end[BOTTOM + pair] = leaving
+                await_end(*row_of(q + 1))
+                await_end(*row_of(q))
+
+            await_end(*row_of(jnp.where(half == 0, q - 1, q + 1)))
+
+        @pl.when(has_prev & jnp.logical_not(apart))
+        def _():
+            @pl.when(first)
+            def _():
+                for early in (0, 1):
+                    await_end(0, early)
+                    await_end(1, early)
+
+            @pl.when(step >= 2)
+            def _():
+                await_end(pair + 1, side)
+
+    def coarse_turn(half, step):
+        pair, side = coarse_at(half, step)
+        slot = slot_of(pair, side)
+        value = conv_relu(field.at[source_at], weights[3], slot, 1)
+
+        def row(ref):
+            return ref[slot].astype(jnp.float32)
+
+        leaving = value + (row(fine) - row(cold))
+        leaving = jnp.where(in_image(pair, side), leaving, 0.0)
+        store(end, slot, 1, leaving)
 
         @pl.when(has_next)
         def _():
-            for side in (0, 1):
-                end_copy(pair, side).start()
+            end_copy(pair, side).start()
 
         @pl.when(pair <= 3)
         def _():
-            end_out[0, 3 - pair], end_out[0, 4 + pair] = leaving
-            coarse_out[0, 3 - pair] = value[:cols].astype(jnp.bfloat16)
-            coarse_out[0, 4 + pair] = value[cols:].astype(jnp.bfloat16)
-
-    @pl.loop(0, last + 1 + lag)
-    def _(turn):
-        @pl.when(turn <= last)
-        def _():
-            @pl.when(turn >= 1)
-            def _():
-                for side in (0, 1):
-                    @pl.when(come[side])
-                    def _(side=side):
-                        field_halo(turn, side).wait_recv()
-
-            fine_step(level0, level1, 0, turn + 2)
-            fine_step(level1, level2, 1, turn + 1)
-            fine_step(level2, fine, 2, turn)
-
-        @pl.when(turn >= lag)
-        def _():
-            coarse_pair(turn - lag)
+            store(end_out.at[0], slot - RIM, 1, leaving)
+            store(coarse_out.at[0], slot - RIM, 1, value)
+
+    @pl.loop(0, halves)
+    def _(half):
+        n_fine = jnp.where(apart, last, 2 * last)
+        n_coarse = jnp.where(half == 0, 8 - 2 * layer, last + layer)
+        n_coarse = jnp.where(apart, n_coarse, 2 * last + 2)
+        lag = jnp.where(layer == 0, jnp.where(half == 0, -2, 0), LAG)
+        lag = jnp.where(layer >= 2, n_fine, lag)
+
+        @pl.loop(0, jnp.maximum(-lag, 0))
+        def _(step):
+            coarse_turn(half, step)
+
+        @pl.loop(0, jnp.maximum(lag, 0))
+        def _(step):
+            await_ring(half, step)
+            fine_turn(half, step)
+
+        @pl.loop(jnp.maximum(lag, 0), n_fine)
+        def _(step):
+            await_ring(half, step)
+            await_entering(half, step - lag)
+            fine_turn(half, step)
+            coarse_turn(half, step - lag)
+
+        @pl.loop(n_fine - lag, n_coarse)
+        def _(step):
+            await_entering(half, step)
+            coarse_turn(half, step)
 
     for side in (0, 1):
         @pl.when(to[side])
@@ -259,13 +324,27 @@
                 end_copy(pair, side).wait_send()
 
 
+def hand_over(end, coarse, end_out, coarse_out, sem):
+    copies = [
+        pltpu.make_async_copy(end, end_out, sem.at[0]),
+        pltpu.make_async_copy(coarse, coarse_out, sem.at[1]),
+    ]
+    for copy in copies:
+        copy.start()
+    for copy in copies:
+        copy.wait()
+
+
 def per_device(states, coarse_old, fine_weights, coarse_weights):
     _, rows, cols, chans = states.shape
     out = jax.ShapeDtypeStruct(states.shape, states.dtype)
     image = (rows + 2 * RIM, cols, chans)
     bf16 = jnp.bfloat16
     dma = pltpu.SemaphoreType.DMA
-    return pl.pallas_call(
+    def stay(array):
+        return pltpu.with_memory_space_constraint(array, pltpu.HBM)
+
+    results = pl.pallas_call(
         kernel,
         out_shape=(out, out),
         in_specs=[pl.BlockSpec(memory_space=pl.ANY)] * 4,
@@ -288,14 +367,22 @@
             dma((2, 7)),
         ],
         compiler_params=pltpu.CompilerParams(
-            vmem_limit_bytes=56 << 20, collective_id=0, has_side_effects=True
+            vmem_limit_bytes=40 << 20, collective_id=0, has_side_effects=True
         ),
     )(
-        states,
-        coarse_old,
-        fine_weights.reshape(1, 3, 3, 3, chans, chans),
-        coarse_weights.reshape(1, 3, 3, chans, chans),
-    )
+        stay(states),
+        stay(coarse_old),
+        stay(fine_weights.reshape(1, 3, 3, 3, chans, chans)),
+        stay(coarse_weights.reshape(1, 3, 3, chans, chans)),
+    )
+    return pl.pallas_call(
+        hand_over,
+        out_shape=(out, out),
+        in_specs=[pl.BlockSpec(memory_space=pl.ANY)] * 2,
+        out_specs=[pl.BlockSpec(memory_space=pl.ANY)] * 2,
+        scratch_shapes=[dma((2,))],
+        compiler_params=pltpu.CompilerParams(vmem_limit_bytes=1 << 20),
+    )(*results)
 
 
 def solution(mesh):

time: 39.6 us -> 35.4 us (0.89); the launches traced: 39.4 us -> 34.7 us
  local copies, waits for them, and re-layouts: 3.74 us -> 0 us
  Pallas kernels: 35 us -> 34.1 us
    unnamed x2 -> x0, local copies, waits for them, and re-layouts: 3.74 us -> none
    pallas_call x1, Pallas kernels: 35 us -> 33.1 us  [per_device(): pl.pallas_call(kernel, out_shape=(out, out), in_specs=[pl.BlockSpec(memor...]
    pallas_call x0 -> x1, Pallas kernels: none -> 0.99 us  [per_device(): pl.pallas_call(hand_over, out_shape=(out, out), in_specs=[pl.BlockSpec(me...]
where the time goes in v2:
time: 35.4 us; the launch traced here: 34.7 us
  Pallas kernels  34.1 us (96%)
  between operations  0.64 us (2%)
    pallas_call x1, Pallas kernels, per_device(): pl.pallas_call(kernel, out_shape=(out, out), in_specs=[pl.BlockSpec(memor...  33.1 us
    pallas_call x1, Pallas kernels, per_device(): pl.pallas_call(hand_over, out_shape=(out, out), in_specs=[pl.BlockSpec(me...  0.99 us

profile of v2, /device:TPU:7, one launch (start us, length us, event | category | flops | bytes accessed | tf_op | source)
XLA Modules:
  0.0 34.7 jit_solution(8496553187661015776)
XLA Ops:
  0.6 33.1 %shard_map.59 = (bf16[1,8,128,256]{3,2,1,0:T(8,128)(2,1)S(1)}, bf16[1,8,128,256]{3,2,1,0:T(8,128)(2,1)S(1)}) custom-call(bf16[1,8,128,256]{3,2,1,0:T(8,128)(2,1)} %states.1, bf16[1,8,128,256]{3,2,1,0:T(8,128)(2,1)} %coarse_old.1, bf16[1,3,3,3,256,256]{5,4,3,2,1,0:T(8,128)(2,1)} %bitcast.2, bf16[1,3,3,256,256]{4,3,2,1,0:T(8,128)(2,1)} %bitcast.3), custom_call_target="tpu_custom_call" | custom-call | tf_op jit(solution)/shard_map/pallas_call | solution.py:347
  33.7 1.0 %shard_map.60 = (bf16[1,8,128,256]{3,2,1,0:T(8,128)(2,1)}, bf16[1,8,128,256]{3,2,1,0:T(8,128)(2,1)}) custom-call(bf16[1,8,128,256]{3,2,1,0:T(8,128)(2,1)S(1)} %get-tuple-element.4.end, bf16[1,8,128,256]{3,2,1,0:T(8,128)(2,1)S(1)} %get-tuple-element.5.coarse), custom_call_target="tpu_custom_call" | custom-call | tf_op jit(solution)/shard_map/pallas_call | solution.py:378

commit v3 on v2

--- a/solution.py
+++ b/solution.py
@@ -9,7 +9,7 @@
 
 RIM = 6
 TOP, BOTTOM = RIM + 3, RIM + 4
-LAG = 2
+LAG = 4
 
 
 def conv_relu(source, weights, start, count):
@@ -36,8 +36,8 @@
 
 
 def kernel(
-    states, coarse_old, fine_w, coarse_w, end_out, coarse_out,
-    field, level1, level2, fine, end, cold, weights,
+    states, coarse_old, fine_w, coarse_w, end, coarse,
+    field, level1, level2, fine, cold, weights,
     load_sem, weight_sem, halo_send, halo_recv, cold_send, cold_recv,
     end_send, end_recv,
 ):
@@ -214,10 +214,16 @@
         def _():
             field_halo(ring, side).wait_recv()
 
-    def fine_turn(half, step):
+    def first_layer(half, step):
         pair, side = fine_at(half, step)
         fine_step(level0, level1, 0, pair + 2, side)
+
+    def second_layer(half, step):
+        pair, side = fine_at(half, step - 1)
         fine_step(level1, level2, 1, pair + 1, side)
+
+    def third_layer(half, step):
+        pair, side = fine_at(half, step - 2)
         fine_step(level2, fine, 2, pair, side)
 
     source_at = jnp.where(has_prev, 1, 0)
@@ -256,7 +262,7 @@
             def _():
                 await_end(pair + 1, side)
 
-    def coarse_turn(half, step):
+    def coarse_row(half, step):
         pair, side = coarse_at(half, step)
         slot = slot_of(pair, side)
         value = conv_relu(field.at[source_at], weights[3], slot, 1)
@@ -265,46 +271,62 @@
             return ref[slot].astype(jnp.float32)
 
         leaving = value + (row(fine) - row(cold))
-        leaving = jnp.where(in_image(pair, side), leaving, 0.0)
-        store(end, slot, 1, leaving)
-
+        store(end, slot, 1, jnp.where(in_image(pair, side), leaving, 0.0))
+        store(coarse, slot, 1, value)
+
+    def send_on(half, step):
         @pl.when(has_next)
         def _():
-            end_copy(pair, side).start()
-
-        @pl.when(pair <= 3)
-        def _():
-            store(end_out.at[0], slot - RIM, 1, leaving)
-            store(coarse_out.at[0], slot - RIM, 1, value)
+            end_copy(*coarse_at(half, step)).start()
 
     @pl.loop(0, halves)
     def _(half):
         n_fine = jnp.where(apart, last, 2 * last)
         n_coarse = jnp.where(half == 0, 8 - 2 * layer, last + layer)
         n_coarse = jnp.where(apart, n_coarse, 2 * last + 2)
-        lag = jnp.where(layer == 0, jnp.where(half == 0, -2, 0), LAG)
-        lag = jnp.where(layer >= 2, n_fine, lag)
-
-        @pl.loop(0, jnp.maximum(-lag, 0))
-        def _(step):
-            coarse_turn(half, step)
-
-        @pl.loop(0, jnp.maximum(lag, 0))
+        lag = jnp.where(layer == 0, jnp.where(half == 0, 0, 2), LAG)
+        lag = jnp.where(layer >= 2, n_fine + 2, lag)
+
+        @pl.loop(0, jnp.minimum(lag, n_fine))
         def _(step):
             await_ring(half, step)
-            fine_turn(half, step)
-
-        @pl.loop(jnp.maximum(lag, 0), n_fine)
+            third_layer(half, step)
+            second_layer(half, step)
+            first_layer(half, step)
+
+        @pl.loop(lag, n_fine)
         def _(step):
             await_ring(half, step)
             await_entering(half, step - lag)
-            fine_turn(half, step)
-            coarse_turn(half, step - lag)
-
-        @pl.loop(n_fine - lag, n_coarse)
+            third_layer(half, step)
+            coarse_row(half, step - lag)
+            second_layer(half, step)
+            first_layer(half, step)
+            send_on(half, step - lag)
+
+        @pl.when(lag <= n_fine)
+        def _():
+            await_entering(half, n_fine - lag)
+            third_layer(half, n_fine)
+            coarse_row(half, n_fine - lag)
+            second_layer(half, n_fine)
+            send_on(half, n_fine - lag)
+            await_entering(half, n_fine + 1 - lag)
+            third_layer(half, n_fine + 1)
+            coarse_row(half, n_fine + 1 - lag)
+            send_on(half, n_fine + 1 - lag)
+
+        @pl.when(lag > n_fine)
+        def _():
+            third_layer(half, n_fine)
+            second_layer(half, n_fine)
+            third_layer(half, n_fine + 1)
+
+        @pl.loop(n_fine + 2 - lag, n_coarse)
         def _(step):
             await_entering(half, step)
-            coarse_turn(half, step)
+            coarse_row(half, step)
+            send_on(half, step)
 
     for side in (0, 1):
         @pl.when(to[side])
@@ -325,9 +347,10 @@
 
 
 def hand_over(end, coarse, end_out, coarse_out, sem):
+    rows = pl.ds(RIM, end_out.shape[1])
     copies = [
-        pltpu.make_async_copy(end, end_out, sem.at[0]),
-        pltpu.make_async_copy(coarse, coarse_out, sem.at[1]),
+        pltpu.make_async_copy(end.at[rows], end_out.at[0], sem.at[0]),
+        pltpu.make_async_copy(coarse.at[rows], coarse_out.at[0], sem.at[1]),
     ]
     for copy in copies:
         copy.start()
@@ -346,12 +369,11 @@
 
     results = pl.pallas_call(
         kernel,
-        out_shape=(out, out),
+        out_shape=(jax.ShapeDtypeStruct(image, bf16),) * 2,
         in_specs=[pl.BlockSpec(memory_space=pl.ANY)] * 4,
         out_specs=[pl.BlockSpec(memory_space=pltpu.VMEM)] * 2,
         scratch_shapes=[
             pltpu.VMEM((2, *image), bf16),
-            pltpu.VMEM(image, bf16),
             pltpu.VMEM(image, bf16),
             pltpu.VMEM(image, bf16),
             pltpu.VMEM(image, bf16),

time: 35.4 us -> 34.5 us (0.975)
  the two profiles are of different devices: /device:TPU:7 before, /device:TPU:27 now
where the time goes in v3:
time: 34.5 us; the launch traced here: 34.4 us
  Pallas kernels  33.8 us (98%)
  between operations  0.64 us (2%)
    pallas_call x1, Pallas kernels, per_device(): pl.pallas_call(kernel, out_shape=(jax.ShapeDtypeStruct(image, bf16),) * 2...  32.8 us
    pallas_call x1, Pallas kernels, per_device(): pl.pallas_call(hand_over, out_shape=(out, out), in_specs=[pl.BlockSpec(me...  0.99 us

profile of v3, /device:TPU:27, one launch (start us, length us, event | category | flops | bytes accessed | tf_op | source)
XLA Modules:
  0.0 34.4 jit_solution(591686735745169400)
XLA Ops:
  0.6 32.8 %shard_map.59 = (bf16[20,128,256]{2,1,0:T(8,128)(2,1)S(1)}, bf16[20,128,256]{2,1,0:T(8,128)(2,1)S(1)}) custom-call(bf16[1,8,128,256]{3,2,1,0:T(8,128)(2,1)} %states.1, bf16[1,8,128,256]{3,2,1,0:T(8,128)(2,1)} %coarse_old.1, bf16[1,3,3,3,256,256]{5,4,3,2,1,0:T(8,128)(2,1)} %bitcast.2, bf16[1,3,3,256,256]{4,3,2,1,0:T(8,128)(2,1)} %bitcast.3), custom_call_target="tpu_custom_call" | custom-call | tf_op jit(solution)/shard_map/pallas_call | solution.py:370
  33.5 1.0 %shard_map.60 = (bf16[1,8,128,256]{3,2,1,0:T(8,128)(2,1)}, bf16[1,8,128,256]{3,2,1,0:T(8,128)(2,1)}) custom-call(bf16[20,128,256]{2,1,0:T(8,128)(2,1)S(1)} %get-tuple-element.4.end, bf16[20,128,256]{2,1,0:T(8,128)(2,1)S(1)} %get-tuple-element.5.coarse), custom_call_target="tpu_custom_call" | custom-call | tf_op jit(solution)/shard_map/pallas_call | solution.py:400

commit v4 on v3

--- a/solution.py
+++ b/solution.py
@@ -39,7 +39,7 @@
     states, coarse_old, fine_w, coarse_w, end, coarse,
     field, level1, level2, fine, cold, weights,
     load_sem, weight_sem, halo_send, halo_recv, cold_send, cold_recv,
-    end_send, end_recv,
+    end_send, end_recv, relay, relay_send, relay_recv, forward_send,
 ):
     layer, space = lax.axis_index("layer"), lax.axis_index("space")
     groups, strips = lax.axis_size("layer"), lax.axis_size("space")
@@ -48,12 +48,18 @@
     has_prev, has_next = layer > 0, layer < groups - 1
     last = groups - 1 - layer + 3
 
+    first_two = layer < 2
+    partner = jnp.where(first_two, layer + 2, layer - 2)
+    relayed = jnp.where(first_two, 3 - layer, 5 - layer)
+    leaves, enters = space == strips // 2 - 1, space == strips // 2
+
     barrier = pltpu.get_barrier_semaphore()
     peers = (
         (has_above, (layer, space - 1)),
         (has_below, (layer, space + 1)),
         (has_prev, (layer - 1, space)),
         (has_next, (layer + 1, space)),
+        (leaves | enters, (partner, space)),
     )
     for present, peer in peers:
         @pl.when(present)
@@ -110,6 +116,45 @@
     def cold_halo(ring, side):
         return halo(ring, side, coarse_old, cold, cold_send, cold_recv)
 
+    def detour(ring, source, target, send, recv, device):
+        return pltpu.make_async_remote_copy(
+            src_ref=source,
+            dst_ref=target,
+            send_sem=send.at[ring - 1],
+            recv_sem=recv,
+            device_id=device,
+            device_id_type=MESH,
+        )
+
+    def to_relay(ring):
+        return detour(
+            ring, coarse_old.at[0, 8 - ring], relay.at[ring - 1],
+            relay_send, relay_recv.at[ring - 1], (partner, space),
+        )
+
+    def over_cut(ring):
+        return detour(
+            ring, relay.at[ring - 1], relay.at[ring - 1],
+            forward_send, relay_recv.at[ring - 1], (layer, space + 1),
+        )
+
+    def from_relay(ring):
+        return detour(
+            ring, relay.at[ring - 1], cold.at[TOP - 3 - ring],
+            forward_send, cold_recv.at[0, ring - 1], (partner, space),
+        )
+
+    def rings(condition, start, stop, act):
+        @pl.when(condition)
+        def _():
+            @pl.loop(start, stop)
+            def _(ring):
+                act(ring)
+
+    relays = leaves & jnp.logical_not(first_two)
+    returns = enters & jnp.logical_not(first_two)
+    detours = leaves & first_two
+
     def end_copy(pair, side):
         slot = slot_of(pair, side)
         return pltpu.make_async_remote_copy(
@@ -150,16 +195,21 @@
         def _():
             pl.semaphore_wait(barrier, greeted)
 
-            for side in (0, 1):
-                @pl.when(to[side])
-                def _(side=side):
-                    @pl.loop(1, last + 1)
-                    def _(ring):
-                        field_halo(ring, side).start()
-
-                    @pl.loop(1, last - 2)
-                    def _(ring):
-                        cold_halo(ring, side).start()
+            def pass_on(ring):
+                to_relay(ring).wait_recv()
+                over_cut(ring).start()
+
+            split = jnp.where(relays, 3, last + 1)
+            rings(detours, 1, relayed + 1, lambda ring: to_relay(ring).start())
+            rings(to[0], 1, split, lambda ring: field_halo(ring, 0).start())
+            rings(to[1], 1, last + 1, lambda ring: field_halo(ring, 1).start())
+            rings(to[1], 1, last - 2, lambda ring: cold_halo(ring, 1).start())
+            rings(relays, 1, relayed + 1, pass_on)
+            rings(to[0], split, last + 1, lambda ring: field_halo(ring, 0).start())
+            rings(
+                to[0] & jnp.logical_not(detours), 1, last - 2,
+                lambda ring: cold_halo(ring, 0).start(),
+            )
 
         @pl.when((part == 0) == late)
         def _():
@@ -281,6 +331,10 @@
 
     @pl.loop(0, halves)
     def _(half):
+        def hand_back(ring):
+            over_cut(ring).wait_recv()
+            from_relay(ring).start()
+
         n_fine = jnp.where(apart, last, 2 * last)
         n_coarse = jnp.where(half == 0, 8 - 2 * layer, last + layer)
         n_coarse = jnp.where(apart, n_coarse, 2 * last + 2)
@@ -322,22 +376,24 @@
             second_layer(half, n_fine)
             third_layer(half, n_fine + 1)
 
+        rings(returns & (half == 0), 1, relayed + 1, hand_back)
+
         @pl.loop(n_fine + 2 - lag, n_coarse)
         def _(step):
             await_entering(half, step)
             coarse_row(half, step)
             send_on(half, step)
 
+    rings(detours, 1, relayed + 1, lambda ring: to_relay(ring).wait_send())
+    rings(relays, 1, relayed + 1, lambda ring: over_cut(ring).wait_send())
+    rings(returns, 1, relayed + 1, lambda ring: from_relay(ring).wait_send())
+    rings(
+        to[0] & jnp.logical_not(detours), 1, last - 2,
+        lambda ring: cold_halo(ring, 0).wait_send(),
+    )
+    rings(to[1], 1, last - 2, lambda ring: cold_halo(ring, 1).wait_send())
     for side in (0, 1):
-        @pl.when(to[side])
-        def _(side=side):
-            @pl.loop(1, last + 1)
-            def _(ring):
-                field_halo(ring, side).wait_send()
-
-            @pl.loop(1, last - 2)
-            def _(ring):
-                cold_halo(ring, side).wait_send()
+        rings(to[side], 1, last + 1, lambda ring, side=side: field_halo(ring, side).wait_send())
 
         @pl.when(has_next)
         def _(side=side):
@@ -387,6 +443,10 @@
             dma((2, 3)),
             dma((2, 7)),
             dma((2, 7)),
+            pltpu.VMEM((3, cols, chans), bf16),
+            dma((3,)),
+            dma((3,)),
+            dma((3,)),
         ],
         compiler_params=pltpu.CompilerParams(
             vmem_limit_bytes=40 << 20, collective_id=0, has_side_effects=True

time: 34.5 us -> 32.7 us (0.948)
  the two profiles are of different devices: /device:TPU:27 before, /device:TPU:7 now
where the time goes in v4:
time: 32.7 us; the launch traced here: 32.1 us
  Pallas kernels  31.5 us (96%)
  between operations  0.64 us (2%)
    pallas_call x1, Pallas kernels, per_device(): pl.pallas_call(kernel, out_shape=(jax.ShapeDtypeStruct(image, bf16),) * 2...  30.5 us
    pallas_call x1, Pallas kernels, per_device(): pl.pallas_call(hand_over, out_shape=(out, out), in_specs=[pl.BlockSpec(me...  0.99 us

profile of v4, /device:TPU:7, one launch (start us, length us, event | category | flops | bytes accessed | tf_op | source)
XLA Modules:
  0.0 32.1 jit_solution(5032033241162405341)
XLA Ops:
  0.6 30.5 %shard_map.59 = (bf16[20,128,256]{2,1,0:T(8,128)(2,1)S(1)}, bf16[20,128,256]{2,1,0:T(8,128)(2,1)S(1)}) custom-call(bf16[1,8,128,256]{3,2,1,0:T(8,128)(2,1)} %states.1, bf16[1,8,128,256]{3,2,1,0:T(8,128)(2,1)} %coarse_old.1, bf16[1,3,3,3,256,256]{5,4,3,2,1,0:T(8,128)(2,1)} %bitcast.2, bf16[1,3,3,256,256]{4,3,2,1,0:T(8,128)(2,1)} %bitcast.3), custom_call_target="tpu_custom_call" | custom-call | tf_op jit(solution)/shard_map/pallas_call | solution.py:426
  31.1 1.0 %shard_map.60 = (bf16[1,8,128,256]{3,2,1,0:T(8,128)(2,1)}, bf16[1,8,128,256]{3,2,1,0:T(8,128)(2,1)}) custom-call(bf16[20,128,256]{2,1,0:T(8,128)(2,1)S(1)} %get-tuple-element.4.end, bf16[20,128,256]{2,1,0:T(8,128)(2,1)S(1)} %get-tuple-element.5.coarse), custom_call_target="tpu_custom_call" | custom-call | tf_op jit(solution)/shard_map/pallas_call | solution.py:460

commit v5 on v4

--- a/solution.py
+++ b/solution.py
@@ -186,8 +186,6 @@
         field[0, RIM + 8 :] = jnp.zeros((RIM, *field.shape[2:]), field.dtype)
 
     level0 = field.at[0]
-    late_above = has_above & (space % 8 <= 1) & (space > 1)
-    late_below = has_below & (space % 8 == 7)
     late = has_above & (space % 8 == 0)
 
     def prelude(part, carry):
@@ -200,14 +198,14 @@
                 over_cut(ring).start()
 
             split = jnp.where(relays, 3, last + 1)
-            rings(detours, 1, relayed + 1, lambda ring: to_relay(ring).start())
+            rings(detours, 2, relayed + 1, lambda ring: to_relay(ring).start())
             rings(to[0], 1, split, lambda ring: field_halo(ring, 0).start())
             rings(to[1], 1, last + 1, lambda ring: field_halo(ring, 1).start())
             rings(to[1], 1, last - 2, lambda ring: cold_halo(ring, 1).start())
-            rings(relays, 1, relayed + 1, pass_on)
+            rings(relays, 2, relayed + 1, pass_on)
             rings(to[0], split, last + 1, lambda ring: field_halo(ring, 0).start())
             rings(
-                to[0] & jnp.logical_not(detours), 1, last - 2,
+                to[0], jnp.where(detours, 1, 1), jnp.where(detours, 2, last - 2),
                 lambda ring: cold_halo(ring, 0).start(),
             )
 
@@ -233,24 +231,27 @@
 
     lax.fori_loop(0, 2, prelude, 0)
 
-    apart = late_above | late_below
-    late_side = late_below.astype(jnp.int32)
+    apart = enters | (space == strips // 2 + 1)
     halves = jnp.where(apart, 2, 1)
+    swap = (space % 8 <= 1).astype(jnp.int32)
 
     def row_of(q):
-        return jnp.where(q >= 0, q, -1 - q), jnp.where(q >= 0, late_side, 1 - late_side)
+        return jnp.where(q >= 0, q, -1 - q), jnp.where(q >= 0, 0, 1)
 
     def fine_at(half, step):
         _, side = row_of(jnp.where(half == 0, -1, 0))
         pair = jnp.where(apart, step, step // 2) + 1
-        return pair, jnp.where(apart, side, step % 2)
+        return pair, jnp.where(apart, side, (step + swap) % 2)
 
     def coarse_q(half, step):
         return jnp.where(half == 0, -layer - step, step - layer + 1)
 
     def coarse_at(half, step):
         pair, side = row_of(coarse_q(half, step))
-        return jnp.where(apart, pair, step // 2), jnp.where(apart, side, step % 2)
+        return (
+            jnp.where(apart, pair, step // 2),
+            jnp.where(apart, side, (step + swap) % 2),
+        )
 
     def fine_step(source, target, which, pair, side):
         slot = slot_of(pair, side)
@@ -338,7 +339,7 @@
         n_fine = jnp.where(apart, last, 2 * last)
         n_coarse = jnp.where(half == 0, 8 - 2 * layer, last + layer)
         n_coarse = jnp.where(apart, n_coarse, 2 * last + 2)
-        lag = jnp.where(layer == 0, jnp.where(half == 0, 0, 2), LAG)
+        lag = jnp.where(half == 0, jnp.where(layer == 0, 0, LAG), 2)
         lag = jnp.where(layer >= 2, n_fine + 2, lag)
 
         @pl.loop(0, jnp.minimum(lag, n_fine))
@@ -376,7 +377,7 @@
             second_layer(half, n_fine)
             third_layer(half, n_fine + 1)
 
-        rings(returns & (half == 0), 1, relayed + 1, hand_back)
+        rings(returns & (half == 0), 2, relayed + 1, hand_back)
 
         @pl.loop(n_fine + 2 - lag, n_coarse)
         def _(step):
@@ -384,11 +385,11 @@
             coarse_row(half, step)
             send_on(half, step)
 
-    rings(detours, 1, relayed + 1, lambda ring: to_relay(ring).wait_send())
-    rings(relays, 1, relayed + 1, lambda ring: over_cut(ring).wait_send())
-    rings(returns, 1, relayed + 1, lambda ring: from_relay(ring).wait_send())
+    rings(detours, 2, relayed + 1, lambda ring: to_relay(ring).wait_send())
+    rings(relays, 2, relayed + 1, lambda ring: over_cut(ring).wait_send())
+    rings(returns, 2, relayed + 1, lambda ring: from_relay(ring).wait_send())
     rings(
-        to[0] & jnp.logical_not(detours), 1, last - 2,
+        to[0], jnp.where(detours, 1, 1), jnp.where(detours, 2, last - 2),
         lambda ring: cold_halo(ring, 0).wait_send(),
     )
     rings(to[1], 1, last - 2, lambda ring: cold_halo(ring, 1).wait_send())

time: 32.7 us -> 31.7 us (0.969); the launches traced: 32.1 us -> 31.6 us
  Pallas kernels: 31.5 us -> 31 us
    pallas_call x1, Pallas kernels: 30.5 us -> 30 us  [per_device(): pl.pallas_call(kernel, out_shape=(jax.ShapeDtypeStruct(image, bf16),) * 2...]
where the time goes in v5:
time: 31.7 us; the launch traced here: 31.6 us
  Pallas kernels  31 us (98%)
  between operations  0.64 us (2%)
    pallas_call x1, Pallas kernels, per_device(): pl.pallas_call(kernel, out_shape=(jax.ShapeDtypeStruct(image, bf16),) * 2...  30 us
    pallas_call x1, Pallas kernels, per_device(): pl.pallas_call(hand_over, out_shape=(out, out), in_specs=[pl.BlockSpec(me...  0.99 us

profile of v5, /device:TPU:7, one launch (start us, length us, event | category | flops | bytes accessed | tf_op | source)
XLA Modules:
  0.0 31.6 jit_solution(18415231743621074891)
XLA Ops:
  0.6 30.0 %shard_map.59 = (bf16[20,128,256]{2,1,0:T(8,128)(2,1)S(1)}, bf16[20,128,256]{2,1,0:T(8,128)(2,1)S(1)}) custom-call(bf16[1,8,128,256]{3,2,1,0:T(8,128)(2,1)} %states.1, bf16[1,8,128,256]{3,2,1,0:T(8,128)(2,1)} %coarse_old.1, bf16[1,3,3,3,256,256]{5,4,3,2,1,0:T(8,128)(2,1)} %bitcast.2, bf16[1,3,3,256,256]{4,3,2,1,0:T(8,128)(2,1)} %bitcast.3), custom_call_target="tpu_custom_call" | custom-call | tf_op jit(solution)/shard_map/pallas_call | solution.py:427
  30.6 1.0 %shard_map.60 = (bf16[1,8,128,256]{3,2,1,0:T(8,128)(2,1)}, bf16[1,8,128,256]{3,2,1,0:T(8,128)(2,1)}) custom-call(bf16[20,128,256]{2,1,0:T(8,128)(2,1)S(1)} %get-tuple-element.4.end, bf16[20,128,256]{2,1,0:T(8,128)(2,1)S(1)} %get-tuple-element.5.coarse), custom_call_target="tpu_custom_call" | custom-call | tf_op jit(solution)/shard_map/pallas_call | solution.py:461

commit v6 on v5

--- a/solution.py
+++ b/solution.py
@@ -151,6 +151,11 @@
             def _(ring):
                 act(ring)
 
+    def send_cold(condition):
+        stop = jnp.where(detours, 2, last - 2)
+        rings(to[0] & condition, 1, stop, lambda ring: cold_halo(ring, 0).start())
+        rings(to[1] & condition, 1, last - 2, lambda ring: cold_halo(ring, 1).start())
+
     relays = leaves & jnp.logical_not(first_two)
     returns = enters & jnp.logical_not(first_two)
     detours = leaves & first_two
@@ -201,13 +206,9 @@
             rings(detours, 2, relayed + 1, lambda ring: to_relay(ring).start())
             rings(to[0], 1, split, lambda ring: field_halo(ring, 0).start())
             rings(to[1], 1, last + 1, lambda ring: field_halo(ring, 1).start())
-            rings(to[1], 1, last - 2, lambda ring: cold_halo(ring, 1).start())
             rings(relays, 2, relayed + 1, pass_on)
             rings(to[0], split, last + 1, lambda ring: field_halo(ring, 0).start())
-            rings(
-                to[0], jnp.where(detours, 1, 1), jnp.where(detours, 2, last - 2),
-                lambda ring: cold_halo(ring, 0).start(),
-            )
+            send_cold(layer != 1)
 
         @pl.when((part == 0) == late)
         def _():
@@ -348,6 +349,8 @@
             third_layer(half, step)
             second_layer(half, step)
             first_layer(half, step)
+
+        send_cold((layer == 1) & (half == 0))
 
         @pl.loop(lag, n_fine)
         def _(step):

time: 31.7 us -> 31.7 us (level)
  no operation moved by 1% of the time
where the time goes in v6:
time: 31.7 us; the launch traced here: 31.5 us
  Pallas kernels  30.9 us (97%)
  between operations  0.64 us (2%)
    pallas_call x1, Pallas kernels, per_device(): pl.pallas_call(kernel, out_shape=(jax.ShapeDtypeStruct(image, bf16),) * 2...  29.9 us
    pallas_call x1, Pallas kernels, per_device(): pl.pallas_call(hand_over, out_shape=(out, out), in_specs=[pl.BlockSpec(me...  0.99 us

profile of v6, /device:TPU:7, one launch (start us, length us, event | category | flops | bytes accessed | tf_op | source)
XLA Modules:
  0.0 31.5 jit_solution(11129816234546597866)
XLA Ops:
  0.6 29.9 %shard_map.59 = (bf16[20,128,256]{2,1,0:T(8,128)(2,1)S(1)}, bf16[20,128,256]{2,1,0:T(8,128)(2,1)S(1)}) custom-call(bf16[1,8,128,256]{3,2,1,0:T(8,128)(2,1)} %states.1, bf16[1,8,128,256]{3,2,1,0:T(8,128)(2,1)} %coarse_old.1, bf16[1,3,3,3,256,256]{5,4,3,2,1,0:T(8,128)(2,1)} %bitcast.2, bf16[1,3,3,256,256]{4,3,2,1,0:T(8,128)(2,1)} %bitcast.3), custom_call_target="tpu_custom_call" | custom-call | tf_op jit(solution)/shard_map/pallas_call | solution.py:430
  30.5 1.0 %shard_map.60 = (bf16[1,8,128,256]{3,2,1,0:T(8,128)(2,1)}, bf16[1,8,128,256]{3,2,1,0:T(8,128)(2,1)}) custom-call(bf16[20,128,256]{2,1,0:T(8,128)(2,1)S(1)} %get-tuple-element.4.end, bf16[20,128,256]{2,1,0:T(8,128)(2,1)S(1)} %get-tuple-element.5.coarse), custom_call_target="tpu_custom_call" | custom-call | tf_op jit(solution)/shard_map/pallas_call | solution.py:464
